TPU v7x, 32 devices: a whole 2x2x4 slice. The times are simulated.
32 devices in a mesh: grp: 2 (over x), col: 16 (over z, y, core).
Axes of the slice: x: 2, y: 2, z: 4, core: 2. Of those that a mesh axis runs over, the one named last changes fastest.
Arguments:
- mode_rows: float32 [16384, 256], P(('grp', 'col')), parts along dimension 0, may hold values from -8 to 8, as said below
- coeffs: bfloat16 [512, 256], P(('grp', 'col')), parts along dimension 0, may hold values from -18 to 18, as said below
- diffusivity: float32 [32, 64], P(('grp', 'col')), parts along dimension 0, may hold values from 0.02 to 0.24
- counts: int32 [32], P(('grp', 'col')), parts along dimension 0, may hold values from 32 to 64
- emis_idx: int32 [512], P('grp'), parts along dimension 0, may hold values from 0 to 15
- emis_table: float32 [16, 8], replicated, may hold values from 0.2 to 1.5
- reactants: int32 [12, 2], replicated, may hold values from 0 to 7
- stoich: int32 [12, 8], replicated, may hold values from -1 to 1
- rate_consts: float32 [12], replicated, may hold values from 0.02 to 0.2
- loss_rates: float32 [8], replicated, may hold values from 0.2 to 2
Outputs:
- modes_out: float32 [16384, 256], P(('grp', 'col')), parts along dimension 0
- coeffs_out: bfloat16 [512, 256], P(('grp', 'col')), parts along dimension 0
There are 2 independent parts, one for each index of `grp`. A program takes and returns all parts, laid end to end along the dimension named above; an argument that names none is the same for every part. Nothing has to cross between parts.
Inputs may be any that keep to these rules, and one draw needn't show every extreme that they name: `mode_rows`: modes of order one. `coeffs`: coefficients of order one.
All inputs are finite; a program needn't handle non-finite values.
Results may differ from a plain program's by a relative error of at most 0.0014.
The roundings to bfloat16 on the way count: a program that leaves them out, or rounds other values in their place, can miss the bound.
Values may be sent and summed in bfloat16 or wider, within the bound.
No kernel may reach another device: no remote copies, remote signals or barrier semaphores. Data moves between devices by JAX's collectives and lax.ppermute only.
A program may use at most 64 MiB of HBM per device.

v0:
```python
import math
import jax
import jax.numpy as jnp
from jax import lax
from jax.sharding import PartitionSpec as P

S = 8
LEV = 64
R = 256
NEMIS = 16
NSUB = 2
TIME_STEP = 0.1
RATE_STEP = 0.3
RIDGE_SHARE = 0.05
PRECISE = lax.Precision.HIGHEST


def diffuse(mode_block, diffusivity, counts):
    ncols = counts.shape[0]
    rank = mode_block.shape[1]
    blocked = mode_block.reshape(ncols, S, LEV, rank)
    level_index = jnp.arange(LEV, dtype=jnp.int32)
    face_coef = jnp.where(
        level_index[None, :] + 1 < counts[:, None], diffusivity, jnp.zeros_like(diffusivity)
    )
    upper_cells = jnp.concatenate([blocked[:, :, 1:], jnp.zeros_like(blocked[:, :, :1])], axis=2)
    face_flux = face_coef[:, None, :, None] * (upper_cells - blocked)
    lower_flux = jnp.concatenate(
        [jnp.zeros_like(face_flux[:, :, :1]), face_flux[:, :, :-1]], axis=2
    )
    return (blocked + face_flux - lower_flux).reshape(mode_block.shape)


def species_pick(table_column):
    return (table_column[:, None] == jnp.arange(S, dtype=jnp.int32)[None, :]).astype(jnp.float32)


def reaction(
    field_block,
    pick_first,
    pick_second,
    stoich_wide,
    rate_consts,
    loss_rates,
    emis_block,
    active,
    profile,
):
    first_amount = jnp.einsum("rs,bcsl->bcrl", pick_first, field_block, precision=PRECISE)
    second_amount = jnp.einsum("rs,bcsl->bcrl", pick_second, field_block, precision=PRECISE)
    reaction_speed = rate_consts[None, None, :, None] * first_amount * second_amount
    produced = jnp.einsum("rs,bcrl->bcsl", stoich_wide, reaction_speed, precision=PRECISE)
    tendency_raw = (
        produced
        - loss_rates[None, None, :, None] * field_block
        + emis_block[:, None, :, None] * profile[None, None, None, :]
    )
    return tendency_raw * active[None, :, None, :]


def on_device(
    mode_rows,
    coeffs,
    diffusivity,
    counts,
    emis_idx,
    emis_table,
    reactants,
    stoich,
    rate_consts,
    loss_rates,
):
    rows_dev = mode_rows.shape[0]
    mem_dev = coeffs.shape[0]
    col_count = lax.axis_size("col")
    total_rows = rows_dev * col_count
    members = mem_dev * col_count
    columns_dev = counts.shape[0]
    level_index = jnp.arange(LEV, dtype=jnp.int32)
    active = (level_index[None, :] < counts[:, None]).astype(jnp.float32)
    profile = jnp.exp(-4.0 * level_index.astype(jnp.float32) / LEV)
    chosen = (emis_idx[:, None] == jnp.arange(NEMIS, dtype=jnp.int32)[None, :]).astype(jnp.float32)
    member_emis = jnp.sum(chosen[:, :, None] * emis_table[None, :, :], axis=1)
    pick_first = species_pick(reactants[:, 0])
    pick_second = species_pick(reactants[:, 1])
    stoich_wide = stoich.astype(jnp.float32)
    rank_root = math.sqrt(R)
    inv_root = 1.0 / rank_root
    block_rows = math.gcd(members, 128)
    block_count = members // block_rows
    modes = mode_rows
    for substep in range(NSUB):
        diffused = diffuse(modes, diffusivity, counts)
        mode_bf = diffused.astype(jnp.bfloat16)
        rate_scale = rank_root / total_rows
        coef_gathered = lax.all_gather(coeffs, "col", axis=0, tiled=True)

        def member_block(pulled, block_inputs):
            coef_block, emis_block = block_inputs
            field_block = (
                lax.dot_general(
                    coef_block,
                    mode_bf,
                    (((1,), (1,)), ((), ())),
                    preferred_element_type=jnp.float32,
                )
                * inv_root
            )
            tendency = reaction(
                field_block.reshape(block_rows, columns_dev, S, LEV),
                pick_first,
                pick_second,
                stoich_wide,
                rate_consts,
                loss_rates,
                emis_block,
                active,
                profile,
            )
            tendency = tendency.reshape(block_rows, rows_dev).astype(jnp.bfloat16)
            pulled = pulled + lax.dot_general(
                tendency, coef_block, (((0,), (0,)), ((), ())), preferred_element_type=jnp.float32
            )
            part_rate = jnp.dot(tendency, mode_bf, preferred_element_type=jnp.float32)
            return (pulled, part_rate)

        pulled, rate_blocks = lax.scan(
            member_block,
            jnp.zeros((rows_dev, R), jnp.float32),
            (
                coef_gathered.reshape(block_count, block_rows, R),
                member_emis.reshape(block_count, block_rows, S),
            ),
        )
        pulled, rate_term = (pulled, rate_blocks.reshape(members, R))
        rate_mine = lax.psum_scatter(rate_term, "col", scatter_dimension=0, tiled=True) * rate_scale
        coef_wide = coeffs.astype(jnp.float32)
        gram_part = jnp.dot(coef_wide.T, coef_wide, precision=PRECISE)
        proj_part = lax.dot_general(
            mode_bf.astype(jnp.float32), pulled, (((0,), (0,)), ((), ())), precision=PRECISE
        )
        gram_matrix, proj_matrix = lax.psum((gram_part, proj_part), "col")
        proj_matrix = proj_matrix / total_rows
        gram_matrix = gram_matrix + RIDGE_SHARE * members * jnp.eye(R, dtype=jnp.float32)
        remainder = pulled - jnp.dot(diffused, proj_matrix, precision=PRECISE)
        factor = jnp.linalg.cholesky(gram_matrix)
        solved = jax.scipy.linalg.cho_solve((factor, True), remainder.T).T
        modes = diffused + TIME_STEP * rank_root * solved
        coeffs = (coef_wide + RATE_STEP * rate_mine).astype(jnp.bfloat16)
    return (modes, coeffs)


def solution(mesh):
    placed = (
        P(("grp", "col"), None),
        P(("grp", "col"), None),
        P(("grp", "col"), None),
        P(("grp", "col")),
        P("grp"),
        P(),
        P(),
        P(),
        P(),
        P(),
    )
    return jax.shard_map(
        on_device,
        mesh=mesh,
        in_specs=placed,
        out_specs=(P(("grp", "col"), None), P(("grp", "col"), None)),
        check_vma=False,
    )
```

profile of v0, /device:TPU:1, one launch (start us, length us, event | category | flops | bytes accessed | tf_op | source)
XLA Modules:
  0.0 393.6 jit_solution(5223242467514382098)
XLA Ops:
  7.2 23.6 %all_gather.6 = bf16[256,256]{1,0:T(8,128)(2,1)S(1)} all-gather(bf16[16,256]{1,0:T(8,128)(2,1)} %param.18), channel_id=1, replica_groups=mesh['grp'=2,'col'=16] {'col'}, dimensions={0}, use_global_device_ids=true | all-gather | bytes 139264 | tf_op jit(solution)/shard_map/all_gather | solution.py:96
  30.8 0.9 fusion.102
  31.7 1.2 slice.80
  34.5 0.7 copy-done.13
  35.2 0.7 copy-done.12
  35.9 0.7 copy-done.10
  38.0 7.1 %while.30 = (s32[]{:T(128)}, f32[512,256]{1,0:T(8,128)S(1)}, f32[2,128,256]{2,1,0:T(8,128)S(1)}, f32[12]{0:T(128)S(1)}, bf16[2,128,256]{2,1,0:T(8,128)(2,1)S(1)}...) while((s32[]{:T(128)}, f32[512,256]{1,0:T(8,128)S(1)}, ...), condition=%wide.region_7.9_spmd.clone, body=%wide.region_6.8_spmd.clone.sunk | while | flops 129892992 | bytes 5650131 | solution.py:127
  38.4 0.7 convolution_bitcast_fusion.10
  39.1 0.7 fusion.186
  39.8 0.7 fusion.187
  41.9 0.7 convolution_bitcast_fusion.10
  42.6 0.7 fusion.186
  45.1 1.2 fusion.103
  46.4 0.7 reduce-scatter.3.cloned.1.call-update
  47.7 86.4 %all-reduce.12.cloned.1.call-done = (f32[256,256]{1,0:T(8,128)}, f32[256,256]{0,1:T(8,128)}) async-done(((f32[256,256]{1,0:T(8,128)}, f32[256,256]{0,1:T(8,128)}), (f32[256,256]{1,0:T(8,128)}, f32[256,256]{0,1:T(8,128)})) %all-reduce.12.cloned.1.call-update) | async-done | bytes 524304 | tf_op jit(solution)/shard_map/psum | solution.py:142
  134.1 1.0 select_add_fusion.1
  135.2 0.8 copy-done.1
  136.1 11.7 %cholesky.130 = f32[128,128]{1,0:T(8,128)S(1)} custom-call(f32[128,128]{1,0:T(8,128)S(1)} %cholesky.194), custom_call_target="Cholesky" | custom-call | tf_op jit(solution)/shard_map/jit(cholesky)/cholesky | solution.py:146
  147.8 9.8 %custom-call.17 = f32[1,128,128]{1,2,0:T(8,128)S(1)} custom-call(f32[1,128,128]{2,1,0:T(8,128)S(1)} %get-tuple-element.369), custom_call_target="InvertDiagBlocksLowerTriangular" | custom-call | tf_op jit(solution)/shard_map/jit(cholesky)/cholesky | solution.py:146
  158.1 11.7 %cholesky.147 = f32[128,128]{1,0:T(8,128)S(1)} custom-call(f32[128,128]{1,0:T(8,128)S(1)} %convolution_subtract_fusion.7), custom_call_target="Cholesky" | custom-call | tf_op jit(solution)/shard_map/jit(cholesky)/cholesky | solution.py:146
  171.9 4.4 %while.32 = (s32[]{:T(128)}, f32[256,256]{1,0:T(8,128)S(1)}, s32[2,2]{1,0:T(2,128)S(1)}, f32[2,128,128]{2,1,0:T(8,128)S(1)}, s32[]{:T(128)}) while((s32[]{:T(128)}, f32[256,256]{1,0:T(8,128)S(1)}, s32[2,2]{1,0:T(2,128)S(1)}, f32[2,128,128]{2,1,0:T(8,128)S(1)}, s32[]{:T(128)}) %tuple.90), condition=%wide.while_cond, body=%wide.while_body.sunk | while | flops 2 | bytes 131181 | solution.py:147
  173.0 1.3 bitcast_dynamic-update-slice_fusion.4
  174.9 1.3 bitcast_dynamic-update-slice_fusion.4
  176.2 19.7 %custom-call.18 = f32[2,128,128]{1,2,0:T(8,128)S(1)} custom-call(f32[2,128,128]{2,1,0:T(8,128)S(1)} %get-tuple-element.258), custom_call_target="InvertDiagBlocksLowerTriangular" | custom-call | tf_op jit(solution)/shard_map/jit(_cho_solve)/triangular_solve | solution.py:147
  199.9 0.7 add_convert_fusion.1
  200.6 21.0 %all_gather.7 = bf16[256,256]{1,0:T(8,128)(2,1)S(1)} all-gather(bf16[16,256]{1,0:T(8,128)(2,1)S(1)} %add_convert_fusion.1), channel_id=1, replica_groups=mesh['grp'=2,'col'=16] {'col'}, dimensions={0}, use_global_device_ids=true | all-gather | bytes 139264 | tf_op jit(solution)/shard_map/all_gather | solution.py:96
  221.7 0.9 fusion.104
  222.6 7.1 %while.31 = (s32[]{:T(128)}, f32[512,256]{1,0:T(8,128)S(1)}, f32[2,128,256]{2,1,0:T(8,128)S(1)}, f32[12]{0:T(128)S(1)}, bf16[2,128,256]{2,1,0:T(8,128)(2,1)S(1)}...) while((s32[]{:T(128)}, f32[512,256]{1,0:T(8,128)S(1)}, ...), condition=%wide.region_12.15_spmd.clone, body=%wide.region_11.14_spmd.clone.sunk | while | flops 129892992 | bytes 5650131 | solution.py:127
  223.0 0.7 convolution_bitcast_fusion.11
  223.7 0.7 fusion.202
  224.4 0.7 fusion.203
  226.5 0.7 convolution_bitcast_fusion.11
  227.2 0.7 fusion.202
  227.9 0.7 fusion.203
  229.7 1.2 fusion.105
  231.5 87.1 %all-reduce.10.cloned.1.call-done = (f32[256,256]{1,0:T(8,128)}, f32[256,256]{0,1:T(8,128)}) async-done(((f32[256,256]{1,0:T(8,128)}, f32[256,256]{0,1:T(8,128)}), (f32[256,256]{1,0:T(8,128)}, f32[256,256]{0,1:T(8,128)})) %all-reduce.10.cloned.1.call-update) | async-done | bytes 524304 | tf_op jit(solution)/shard_map/psum | solution.py:142
  318.6 1.0 select_add_fusion
  319.8 0.8 copy-done.2
  320.6 11.7 %cholesky.164 = f32[128,128]{1,0:T(8,128)S(1)} custom-call(f32[128,128]{1,0:T(8,128)S(1)} %cholesky.197), custom_call_target="Cholesky" | custom-call | tf_op jit(solution)/shard_map/jit(cholesky)/cholesky | solution.py:146
  332.4 9.8 %custom-call.19 = f32[1,128,128]{1,2,0:T(8,128)S(1)} custom-call(f32[1,128,128]{2,1,0:T(8,128)S(1)} %get-tuple-element.365), custom_call_target="InvertDiagBlocksLowerTriangular" | custom-call | tf_op jit(solution)/shard_map/jit(cholesky)/cholesky | solution.py:146
  342.7 11.7 %cholesky.181 = f32[128,128]{1,0:T(8,128)S(1)} custom-call(f32[128,128]{1,0:T(8,128)S(1)} %convolution_subtract_fusion.6), custom_call_target="Cholesky" | custom-call | tf_op jit(solution)/shard_map/jit(cholesky)/cholesky | solution.py:146
  354.4 0.7 compare_reduce_fusion
  357.2 4.3 %while.33 = (s32[]{:T(128)}, f32[256,256]{1,0:T(8,128)S(1)}, s32[2,2]{1,0:T(2,128)S(1)}, f32[2,128,128]{2,1,0:T(8,128)S(1)}, s32[]{:T(128)}) while((s32[]{:T(128)}, f32[256,256]{1,0:T(8,128)S(1)}, s32[2,2]{1,0:T(2,128)S(1)}, f32[2,128,128]{2,1,0:T(8,128)S(1)}, s32[]{:T(128)}) %tuple.120), condition=%wide.while_cond.clone, body=%wide.while_body.clone.sunk | while | flops 2 | bytes 131181 | solution.py:147
  358.0 1.4 bitcast_dynamic-update-slice_fusion.5
  360.1 1.4 bitcast_dynamic-update-slice_fusion.5
  361.5 19.7 %custom-call.20 = f32[2,128,128]{1,2,0:T(8,128)S(1)} custom-call(f32[2,128,128]{2,1,0:T(8,128)S(1)} %get-tuple-element.259), custom_call_target="InvertDiagBlocksLowerTriangular" | custom-call | tf_op jit(solution)/shard_map/jit(_cho_solve)/triangular_solve | solution.py:147
  384.5 1.0 copy.72
  385.5 1.3 add_convert_fusion
  (135 shorter events, 22.4 us)
Async XLA Ops:
  7.2 126.9 %all-reduce.12.cloned.1.call-start = ((), (), s32[]{:S(2)}) async-start(), calls=%async_computation.5 | async-start | bytes 1048576 | tf_op jit(solution)/shard_map/psum | solution.py:142
  7.2 23.6 %copy-start.7 = (bf16[16,256]{1,0:T(8,128)(2,1)S(1)}, bf16[16,256]{1,0:T(8,128)(2,1)}, u32[]{:S(2)}) copy-start(bf16[16,256]{1,0:T(8,128)(2,1)} %param.18) | copy-start | bytes 24580
  31.7 2.5 copy-start
  33.6 0.7 copy-start.14
  34.5 0.7 copy-start.13
  35.2 0.7 copy-start.12
  35.9 0.7 copy-start.10
  36.6 0.7 copy-start.11
  37.4 0.7 copy-start.8
  37.4 0.7 copy-start.9
  45.1 1.2 copy-start.3
  46.3 153.5 %reduce-scatter.3.cloned.1.call-start = ((), (), s32[]{:S(2)}) async-start(), calls=%async_computation.2 | async-start | bytes 278528 | tf_op jit(solution)/shard_map/reduce_scatter | solution.py:136
  47.1 271.5 %all-reduce.10.cloned.1.call-start = ((), (), s32[]{:S(2)}) async-start(), calls=%async_computation.4 | async-start | bytes 1048576 | tf_op jit(solution)/shard_map/psum | solution.py:142
  135.1 1.0 copy-start.1
  171.9 24.1 %copy-start.5 = (f32[256,256]{1,0:T(8,128)S(1)}, f32[256,256]{1,0:T(8,128)}, u32[]{:S(2)}) copy-start(f32[256,256]{1,0:T(8,128)} %get-tuple-element.356) | copy-start | bytes 786436
  229.7 1.2 copy-start.4
  230.9 154.6 %reduce-scatter.5.cloned.1.call-start = ((), (), s32[]{:S(2)}) async-start(), calls=%async_computation.3 | async-start | bytes 278528 | tf_op jit(solution)/shard_map/reduce_scatter | solution.py:136
  319.6 1.0 copy-start.2
  357.2 24.0 %copy-start.6 = (f32[256,256]{1,0:T(8,128)S(1)}, f32[256,256]{1,0:T(8,128)}, u32[]{:S(2)}) copy-start(f32[256,256]{1,0:T(8,128)} %get-tuple-element.354) | copy-start | bytes 786436
Sparse Core Ops, SparseCore 0:
  46.5 87.5 all-reduce.11
  137.6 53.6 reduce-scatter.2
  231.0 87.5 all-reduce.9
  322.0 53.5 reduce-scatter.4
where the time goes:
time: 398 us; the launch traced here: 394 us
  waiting for transfers between devices  174 us (44%)
  other arithmetic  116 us (29%)
  blocking collectives  44.6 us (11%)
  matrix products  22 us (6%)
  between operations  17.7 us (4%)
  local copies, waits for them, and re-layouts  17.3 us (4%)
    psum x2, waiting for transfers between devices, on_device(): gram_matrix, proj_matrix = lax.psum((gram_part, proj_part), 'col')  174 us
    another operation x13, other arithmetic, on_device(): factor = jnp.linalg.cholesky(gram_matrix)  68.6 us
    all_gather x2, blocking collectives, on_device(): coef_gathered = lax.all_gather(coeffs, 'col', axis=0, tiled=True)  44.6 us
    another operation x5, other arithmetic, on_device(): solved = jax.scipy.linalg.cho_solve((factor, True), remainder.T).T  39.4 us
  transfers between devices with their start and end apart: 4, of which 2 were waited for; matrix products, arithmetic and copies ran while one was open for 32% of the time, Pallas kernels for 0%

commit v1 on v0

--- a/solution.py
+++ b/solution.py
@@ -13,6 +13,12 @@
 RATE_STEP = 0.3
 RIDGE_SHARE = 0.05
 PRECISE = lax.Precision.HIGHEST
+
+
+def laid_out(blocks, dim):
+    blocks = jnp.moveaxis(blocks, 0, dim)
+    dims = blocks.shape
+    return blocks.reshape(*dims[:dim], dims[dim] * dims[dim + 1], *dims[dim + 2 :])
 
 
 def diffuse(mode_block, diffusivity, counts):
@@ -93,7 +99,19 @@
         diffused = diffuse(modes, diffusivity, counts)
         mode_bf = diffused.astype(jnp.bfloat16)
         rate_scale = rank_root / total_rows
-        coef_gathered = lax.all_gather(coeffs, "col", axis=0, tiled=True)
+        length = lax.axis_size("col")
+        pairs = [(i, (i + 1) % length) for i in range(length)]
+        back = [(b, a) for a, b in pairs]
+        lower, upper = ([], [])
+        for lap in range(length - 1):
+            if lap % 2 == 0:
+                lower.append(lax.ppermute(lower[-1] if lower else coeffs, "col", pairs))
+            else:
+                upper.append(lax.ppermute(upper[-1] if upper else coeffs, "col", back))
+        blocks = jnp.stack([*lower[::-1], coeffs, *upper])
+        shift = lax.axis_index("col") - len(lower)
+        blocks = blocks[(jnp.arange(length) - shift) % length]
+        coef_gathered = laid_out(blocks, 0)
 
         def member_block(pulled, block_inputs):
             coef_block, emis_block = block_inputs

time: 398 us -> 450 us (1.13)
  starting transfers between devices: 0.62 us -> 70 us
  blocking collectives: 44.6 us -> 0 us
  waiting for transfers between devices: 174 us -> 203 us
    ppermute x0 -> x30, starting transfers between devices: none -> 69.1 us  [the longest x14 61 us: on_device(): upper.append(lax.ppermute(upper[-1] if upper else coeffs, 'col', back))]
    all_gather x2 -> x0, blocking collectives: 44.6 us -> none  [on_device(): coef_gathered = lax.all_gather(coeffs, 'col', axis=0, tiled=True)]
    psum x2, waiting for transfers between devices: 174 us -> 191 us  [on_device(): gram_matrix, proj_matrix = lax.psum((gram_part, proj_part), 'col')]
    ppermute x0 -> x30, waiting for transfers between devices: none -> 10.9 us  [the longest x14 7.54 us: on_device(): upper.append(lax.ppermute(upper[-1] if upper else coeffs, 'col', back))]
  transfers between devices with their start and end apart: 4 -> 34, of which waited for: 2 -> 22; matrix products, arithmetic and copies ran while one was open for 32% -> 30% of each run, Pallas kernels for 0% -> 0%
where the time goes in v1:
time: 450 us; the launch traced here: 445 us
  waiting for transfers between devices  203 us (45%)
  other arithmetic  116 us (26%)
  starting transfers between devices  70 us (16%)
  matrix products  22 us (5%)
  between operations  18.2 us (4%)
  local copies, waits for them, and re-layouts  16.1 us (4%)
    psum x2, waiting for transfers between devices, on_device(): gram_matrix, proj_matrix = lax.psum((gram_part, proj_part), 'col')  191 us
    another operation x13, other arithmetic, on_device(): factor = jnp.linalg.cholesky(gram_matrix)  68.7 us
    ppermute x14, starting transfers between devices, on_device(): upper.append(lax.ppermute(upper[-1] if upper else coeffs, 'col', back))  61 us
    another operation x5, other arithmetic, on_device(): solved = jax.scipy.linalg.cho_solve((factor, True), remainder.T).T  39.4 us
  transfers between devices with their start and end apart: 34, of which 22 were waited for; matrix products, arithmetic and copies ran while one was open for 30% of the time, Pallas kernels for 0%

profile of v1, /device:TPU:1, one launch (start us, length us, event | category | flops | bytes accessed | tf_op | source)
XLA Modules:
  0.0 445.5 jit_solution(14666413045978697926)
XLA Ops:
  7.2 2.7 collective-permute-start
  9.9 1.2 slice.84
  12.7 1.8 collective-permute-start.1
  14.5 1.8 collective-permute-done.1
  16.3 1.2 collective-permute-start.2
  17.5 0.9 fusion.104
  18.5 3.9 collective-permute-start.9
  23.2 5.0 %collective-permute-start.10 = (bf16[16,256]{1,0:T(8,128)(2,1)S(1)}, bf16[16,256]{1,0:T(8,128)(2,1)S(1)}, u32[]{:S(2)}, u32[]{:S(2)}) collective-permute-start(bf16[16,256]{1,0:T(8,128)(2,1)S(1)} %collective-permute-done.9), channel_id=1, source_target_pairs={{1,0},{2,1},{3,2},{4,3},{5,4},{6,5},{7,6},{8,7},{9,8},{10,9},{11,1... | collective-permute-start | bytes 24584 | tf_op jit(solution)/shard_map/ppermute | solution.py:110
  29.0 4.9 %collective-permute-start.11 = (bf16[16,256]{1,0:T(8,128)(2,1)S(1)}, bf16[16,256]{1,0:T(8,128)(2,1)S(1)}, u32[]{:S(2)}, u32[]{:S(2)}) collective-permute-start(bf16[16,256]{1,0:T(8,128)(2,1)S(1)} %collective-permute-done.10), channel_id=1, source_target_pairs={{1,0},{2,1},{3,2},{4,3},{5,4},{6,5},{7,6},{8,7},{9,8},{10,9},{11,1... | collective-permute-start | bytes 24584 | tf_op jit(solution)/shard_map/ppermute | solution.py:110
  34.8 4.9 %collective-permute-start.12 = (bf16[16,256]{1,0:T(8,128)(2,1)S(1)}, bf16[16,256]{1,0:T(8,128)(2,1)S(1)}, u32[]{:S(2)}, u32[]{:S(2)}) collective-permute-start(bf16[16,256]{1,0:T(8,128)(2,1)S(1)} %collective-permute-done.11), channel_id=1, source_target_pairs={{1,0},{2,1},{3,2},{4,3},{5,4},{6,5},{7,6},{8,7},{9,8},{10,9},{11,1... | collective-permute-start | bytes 24584 | tf_op jit(solution)/shard_map/ppermute | solution.py:110
  39.7 0.8 collective-permute-done.12
  40.5 4.9 %collective-permute-start.13 = (bf16[16,256]{1,0:T(8,128)(2,1)S(1)}, bf16[16,256]{1,0:T(8,128)(2,1)S(1)}, u32[]{:S(2)}, u32[]{:S(2)}) collective-permute-start(bf16[16,256]{1,0:T(8,128)(2,1)S(1)} %collective-permute-done.12), channel_id=1, source_target_pairs={{1,0},{2,1},{3,2},{4,3},{5,4},{6,5},{7,6},{8,7},{9,8},{10,9},{11,1... | collective-permute-start | bytes 24584 | tf_op jit(solution)/shard_map/ppermute | solution.py:110
  46.3 4.9 %collective-permute-start.14 = (bf16[16,256]{1,0:T(8,128)(2,1)S(1)}, bf16[16,256]{1,0:T(8,128)(2,1)S(1)}, u32[]{:S(2)}, u32[]{:S(2)}) collective-permute-start(bf16[16,256]{1,0:T(8,128)(2,1)S(1)} %collective-permute-done.13), channel_id=1, source_target_pairs={{1,0},{2,1},{3,2},{4,3},{5,4},{6,5},{7,6},{8,7},{9,8},{10,9},{11,1... | collective-permute-start | bytes 24584 | tf_op jit(solution)/shard_map/ppermute | solution.py:110
  53.3 7.1 %while.30 = (s32[]{:T(128)}, f32[512,256]{1,0:T(8,128)S(1)}, f32[2,128,256]{2,1,0:T(8,128)S(1)}, f32[12]{0:T(128)S(1)}, bf16[2,128,256]{2,1,0:T(8,128)(2,1)S(1)}...) while((s32[]{:T(128)}, f32[512,256]{1,0:T(8,128)S(1)}, ...), condition=%wide.region_7.9_spmd.clone, body=%wide.region_6.8_spmd.clone.sunk | while | flops 129892992 | bytes 5650131 | solution.py:145
  60.4 1.2 fusion.105
  63.0 95.4 %all-reduce.12.cloned.1.call-done = (f32[256,256]{1,0:T(8,128)}, f32[256,256]{0,1:T(8,128)}) async-done(((f32[256,256]{1,0:T(8,128)}, f32[256,256]{0,1:T(8,128)}), (f32[256,256]{1,0:T(8,128)}, f32[256,256]{0,1:T(8,128)})) %all-reduce.12.cloned.1.call-update) | async-done | bytes 524304 | tf_op jit(solution)/shard_map/psum | solution.py:160
  158.4 1.0 select_add_fusion.1
  159.5 0.8 copy-done.1
  160.4 11.7 %cholesky.130 = f32[128,128]{1,0:T(8,128)S(1)} custom-call(f32[128,128]{1,0:T(8,128)S(1)} %cholesky.194), custom_call_target="Cholesky" | custom-call | tf_op jit(solution)/shard_map/jit(cholesky)/cholesky | solution.py:164
  172.1 9.8 %custom-call.17 = f32[1,128,128]{1,2,0:T(8,128)S(1)} custom-call(f32[1,128,128]{2,1,0:T(8,128)S(1)} %get-tuple-element.369), custom_call_target="InvertDiagBlocksLowerTriangular" | custom-call | tf_op jit(solution)/shard_map/jit(cholesky)/cholesky | solution.py:164
  182.4 11.7 %cholesky.147 = f32[128,128]{1,0:T(8,128)S(1)} custom-call(f32[128,128]{1,0:T(8,128)S(1)} %convolution_subtract_fusion.7), custom_call_target="Cholesky" | custom-call | tf_op jit(solution)/shard_map/jit(cholesky)/cholesky | solution.py:164
  196.4 4.2 while.32
  197.1 1.4 bitcast_dynamic-update-slice_fusion.4
  199.2 1.4 bitcast_dynamic-update-slice_fusion.4
  200.6 19.7 %custom-call.18 = f32[2,128,128]{1,2,0:T(8,128)S(1)} custom-call(f32[2,128,128]{2,1,0:T(8,128)S(1)} %get-tuple-element.258), custom_call_target="InvertDiagBlocksLowerTriangular" | custom-call | tf_op jit(solution)/shard_map/jit(_cho_solve)/triangular_solve | solution.py:165
  224.3 2.1 collective-permute-start.16
  226.8 2.5 collective-permute-start.23
  230.2 5.0 %collective-permute-start.24 = (bf16[16,256]{1,0:T(8,128)(2,1)S(1)}, bf16[16,256]{1,0:T(8,128)(2,1)S(1)}, u32[]{:S(2)}, u32[]{:S(2)}) collective-permute-start(bf16[16,256]{1,0:T(8,128)(2,1)S(1)} %collective-permute-done.23), channel_id=1, source_target_pairs={{1,0},{2,1},{3,2},{4,3},{5,4},{6,5},{7,6},{8,7},{9,8},{10,9},{11,1... | collective-permute-start | bytes 24584 | tf_op jit(solution)/shard_map/ppermute | solution.py:110
  236.0 4.9 %collective-permute-start.25 = (bf16[16,256]{1,0:T(8,128)(2,1)S(1)}, bf16[16,256]{1,0:T(8,128)(2,1)S(1)}, u32[]{:S(2)}, u32[]{:S(2)}) collective-permute-start(bf16[16,256]{1,0:T(8,128)(2,1)S(1)} %collective-permute-done.24), channel_id=1, source_target_pairs={{1,0},{2,1},{3,2},{4,3},{5,4},{6,5},{7,6},{8,7},{9,8},{10,9},{11,1... | collective-permute-start | bytes 24584 | tf_op jit(solution)/shard_map/ppermute | solution.py:110
  241.7 4.9 %collective-permute-start.26 = (bf16[16,256]{1,0:T(8,128)(2,1)S(1)}, bf16[16,256]{1,0:T(8,128)(2,1)S(1)}, u32[]{:S(2)}, u32[]{:S(2)}) collective-permute-start(bf16[16,256]{1,0:T(8,128)(2,1)S(1)} %collective-permute-done.25), channel_id=1, source_target_pairs={{1,0},{2,1},{3,2},{4,3},{5,4},{6,5},{7,6},{8,7},{9,8},{10,9},{11,1... | collective-permute-start | bytes 24584 | tf_op jit(solution)/shard_map/ppermute | solution.py:110
  247.5 4.9 %collective-permute-start.27 = (bf16[16,256]{1,0:T(8,128)(2,1)S(1)}, bf16[16,256]{1,0:T(8,128)(2,1)S(1)}, u32[]{:S(2)}, u32[]{:S(2)}) collective-permute-start(bf16[16,256]{1,0:T(8,128)(2,1)S(1)} %collective-permute-done.26), channel_id=1, source_target_pairs={{1,0},{2,1},{3,2},{4,3},{5,4},{6,5},{7,6},{8,7},{9,8},{10,9},{11,1... | collective-permute-start | bytes 24584 | tf_op jit(solution)/shard_map/ppermute | solution.py:110
  253.3 4.9 %collective-permute-start.28 = (bf16[16,256]{1,0:T(8,128)(2,1)S(1)}, bf16[16,256]{1,0:T(8,128)(2,1)S(1)}, u32[]{:S(2)}, u32[]{:S(2)}) collective-permute-start(bf16[16,256]{1,0:T(8,128)(2,1)S(1)} %collective-permute-done.27), channel_id=1, source_target_pairs={{1,0},{2,1},{3,2},{4,3},{5,4},{6,5},{7,6},{8,7},{9,8},{10,9},{11,1... | collective-permute-start | bytes 24584 | tf_op jit(solution)/shard_map/ppermute | solution.py:110
  258.4 0.9 fusion.106
  259.3 5.1 %collective-permute-start.29 = (bf16[16,256]{1,0:T(8,128)(2,1)S(1)}, bf16[16,256]{1,0:T(8,128)(2,1)S(1)}, u32[]{:S(2)}, u32[]{:S(2)}) collective-permute-start(bf16[16,256]{1,0:T(8,128)(2,1)S(1)} %collective-permute-done.28), channel_id=1, source_target_pairs={{1,0},{2,1},{3,2},{4,3},{5,4},{6,5},{7,6},{8,7},{9,8},{10,9},{11,1... | collective-permute-start | bytes 24584 | tf_op jit(solution)/shard_map/ppermute | solution.py:110
  265.8 7.1 %while.31 = (s32[]{:T(128)}, f32[512,256]{1,0:T(8,128)S(1)}, f32[2,128,256]{2,1,0:T(8,128)S(1)}, f32[12]{0:T(128)S(1)}, bf16[2,128,256]{2,1,0:T(8,128)(2,1)S(1)}...) while((s32[]{:T(128)}, f32[512,256]{1,0:T(8,128)S(1)}, ...), condition=%wide.region_12.15_spmd.clone, body=%wide.region_11.14_spmd.clone.sunk | while | flops 129892992 | bytes 5650131 | solution.py:145
  272.9 1.2 fusion.107
  274.7 95.8 %all-reduce.10.cloned.1.call-done = (f32[256,256]{1,0:T(8,128)}, f32[256,256]{0,1:T(8,128)}) async-done(((f32[256,256]{1,0:T(8,128)}, f32[256,256]{0,1:T(8,128)}), (f32[256,256]{1,0:T(8,128)}, f32[256,256]{0,1:T(8,128)})) %all-reduce.10.cloned.1.call-update) | async-done | bytes 524304 | tf_op jit(solution)/shard_map/psum | solution.py:160
  370.5 1.0 select_add_fusion
  371.6 0.8 copy-done.2
  372.5 11.7 %cholesky.164 = f32[128,128]{1,0:T(8,128)S(1)} custom-call(f32[128,128]{1,0:T(8,128)S(1)} %cholesky.197), custom_call_target="Cholesky" | custom-call | tf_op jit(solution)/shard_map/jit(cholesky)/cholesky | solution.py:164
  384.3 9.8 %custom-call.19 = f32[1,128,128]{1,2,0:T(8,128)S(1)} custom-call(f32[1,128,128]{2,1,0:T(8,128)S(1)} %get-tuple-element.365), custom_call_target="InvertDiagBlocksLowerTriangular" | custom-call | tf_op jit(solution)/shard_map/jit(cholesky)/cholesky | solution.py:164
  394.5 11.7 %cholesky.181 = f32[128,128]{1,0:T(8,128)S(1)} custom-call(f32[128,128]{1,0:T(8,128)S(1)} %convolution_subtract_fusion.6), custom_call_target="Cholesky" | custom-call | tf_op jit(solution)/shard_map/jit(cholesky)/cholesky | solution.py:164
  409.0 4.3 while.33
  409.9 1.4 bitcast_dynamic-update-slice_fusion.5
  411.9 1.4 bitcast_dynamic-update-slice_fusion.5
  413.3 19.7 %custom-call.20 = f32[2,128,128]{1,2,0:T(8,128)S(1)} custom-call(f32[2,128,128]{2,1,0:T(8,128)S(1)} %get-tuple-element.259), custom_call_target="InvertDiagBlocksLowerTriangular" | custom-call | tf_op jit(solution)/shard_map/jit(_cho_solve)/triangular_solve | solution.py:165
  436.4 1.0 copy.72
  437.4 1.3 add_convert_fusion
  (229 shorter events, 41.0 us)
Async XLA Ops:
  7.2 151.2 %all-reduce.12.cloned.1.call-start = ((), (), s32[]{:S(2)}) async-start(), calls=%async_computation.5 | async-start | bytes 1048576 | tf_op jit(solution)/shard_map/psum | solution.py:160
  7.2 5.4 %collective-permute-start = (bf16[16,256]{1,0:T(8,128)(2,1)}, bf16[16,256]{1,0:T(8,128)(2,1)S(1)}, u32[]{:S(2)}, u32[]{:S(2)}) collective-permute-start(bf16[16,256]{1,0:T(8,128)(2,1)} %param.18), channel_id=1, source_target_pairs={{0,1},{1,2},{2,3},{3,4},{4,5},{5,6},{6,7},{7,8},{8,9},{9,10},{10,1... | collective-permute-start | bytes 24584 | tf_op jit(solution)/shard_map/ppermute | solution.py:108
  9.9 8.6 %collective-permute-start.8 = (bf16[16,256]{1,0:T(8,128)(2,1)}, bf16[16,256]{1,0:T(8,128)(2,1)S(1)}, u32[]{:S(2)}, u32[]{:S(2)}) collective-permute-start(bf16[16,256]{1,0:T(8,128)(2,1)} %param.18), channel_id=1, source_target_pairs={{1,0},{2,1},{3,2},{4,3},{5,4},{6,5},{7,6},{8,7},{9,8},{10,9},{11,1... | collective-permute-start | bytes 24584 | tf_op jit(solution)/shard_map/ppermute | solution.py:110
  9.9 2.5 copy-start
  11.7 0.7 copy-start.14
  12.7 3.7 collective-permute-start.1
  14.4 3.1 copy-start.7
  14.5 7.9 %copy-start.12 = (s32[256]{0:T(256)S(1)}, s32[256]{0:T(256)}, u32[]{:S(2)}) copy-start(s32[256]{0:T(256)} %param.21) | copy-start | bytes 3076
  16.3 6.0 %collective-permute-start.2 = (bf16[16,256]{1,0:T(8,128)(2,1)S(1)}, bf16[16,256]{1,0:T(8,128)(2,1)S(1)}, u32[]{:S(2)}, u32[]{:S(2)}) collective-permute-start(bf16[16,256]{1,0:T(8,128)(2,1)S(1)} %collective-permute-done.1), channel_id=1, source_target_pairs={{0,1},{1,2},{2,3},{3,4},{4,5},{5,6},{6,7},{7,8},{8,9},{9,10},{10,1... | collective-permute-start | bytes 24584 | tf_op jit(solution)/shard_map/ppermute | solution.py:108
  18.5 9.7 %copy-start.13 = (s32[12,2]{0,1:T(2,128)S(1)}, s32[12,2]{0,1:T(2,128)}, u32[]{:S(2)}) copy-start(s32[12,2]{0,1:T(2,128)} %param.23) | copy-start | bytes 292
  18.5 4.7 %collective-permute-start.9 = (bf16[16,256]{1,0:T(8,128)(2,1)S(1)}, bf16[16,256]{1,0:T(8,128)(2,1)S(1)}, u32[]{:S(2)}, u32[]{:S(2)}) collective-permute-start(bf16[16,256]{1,0:T(8,128)(2,1)S(1)} %collective-permute-done.8), channel_id=1, source_target_pairs={{1,0},{2,1},{3,2},{4,3},{5,4},{6,5},{7,6},{8,7},{9,8},{10,9},{11,1... | collective-permute-start | bytes 24584 | tf_op jit(solution)/shard_map/ppermute | solution.py:110
  22.4 5.8 %collective-permute-start.3 = (bf16[16,256]{1,0:T(8,128)(2,1)S(1)}, bf16[16,256]{1,0:T(8,128)(2,1)S(1)}, u32[]{:S(2)}, u32[]{:S(2)}) collective-permute-start(bf16[16,256]{1,0:T(8,128)(2,1)S(1)} %collective-permute-done.2), channel_id=1, source_target_pairs={{0,1},{1,2},{2,3},{3,4},{4,5},{5,6},{6,7},{7,8},{8,9},{9,10},{10,1... | collective-permute-start | bytes 24584 | tf_op jit(solution)/shard_map/ppermute | solution.py:108
  22.4 5.8 %copy-start.10 = (f32[16,8]{0,1:T(8,128)S(1)}, f32[16,8]{0,1:T(8,128)}, u32[]{:S(2)}) copy-start(f32[16,8]{0,1:T(8,128)} %param.22) | copy-start | bytes 1540
  23.2 5.8 %collective-permute-start.10 = (bf16[16,256]{1,0:T(8,128)(2,1)S(1)}, bf16[16,256]{1,0:T(8,128)(2,1)S(1)}, u32[]{:S(2)}, u32[]{:S(2)}) collective-permute-start(bf16[16,256]{1,0:T(8,128)(2,1)S(1)} %collective-permute-done.9), channel_id=1, source_target_pairs={{1,0},{2,1},{3,2},{4,3},{5,4},{6,5},{7,6},{8,7},{9,8},{10,9},{11,1... | collective-permute-start | bytes 24584 | tf_op jit(solution)/shard_map/ppermute | solution.py:110
  28.2 5.8 %collective-permute-start.4 = (bf16[16,256]{1,0:T(8,128)(2,1)S(1)}, bf16[16,256]{1,0:T(8,128)(2,1)S(1)}, u32[]{:S(2)}, u32[]{:S(2)}) collective-permute-start(bf16[16,256]{1,0:T(8,128)(2,1)S(1)} %collective-permute-done.3), channel_id=1, source_target_pairs={{0,1},{1,2},{2,3},{3,4},{4,5},{5,6},{6,7},{7,8},{8,9},{9,10},{10,1... | collective-permute-start | bytes 24584 | tf_op jit(solution)/shard_map/ppermute | solution.py:108
  29.0 5.8 %collective-permute-start.11 = (bf16[16,256]{1,0:T(8,128)(2,1)S(1)}, bf16[16,256]{1,0:T(8,128)(2,1)S(1)}, u32[]{:S(2)}, u32[]{:S(2)}) collective-permute-start(bf16[16,256]{1,0:T(8,128)(2,1)S(1)} %collective-permute-done.10), channel_id=1, source_target_pairs={{1,0},{2,1},{3,2},{4,3},{5,4},{6,5},{7,6},{8,7},{9,8},{10,9},{11,1... | collective-permute-start | bytes 24584 | tf_op jit(solution)/shard_map/ppermute | solution.py:110
  33.9 5.8 %collective-permute-start.5 = (bf16[16,256]{1,0:T(8,128)(2,1)S(1)}, bf16[16,256]{1,0:T(8,128)(2,1)S(1)}, u32[]{:S(2)}, u32[]{:S(2)}) collective-permute-start(bf16[16,256]{1,0:T(8,128)(2,1)S(1)} %collective-permute-done.4), channel_id=1, source_target_pairs={{0,1},{1,2},{2,3},{3,4},{4,5},{5,6},{6,7},{7,8},{8,9},{9,10},{10,1... | collective-permute-start | bytes 24584 | tf_op jit(solution)/shard_map/ppermute | solution.py:108
  34.8 5.8 %collective-permute-start.12 = (bf16[16,256]{1,0:T(8,128)(2,1)S(1)}, bf16[16,256]{1,0:T(8,128)(2,1)S(1)}, u32[]{:S(2)}, u32[]{:S(2)}) collective-permute-start(bf16[16,256]{1,0:T(8,128)(2,1)S(1)} %collective-permute-done.11), channel_id=1, source_target_pairs={{1,0},{2,1},{3,2},{4,3},{5,4},{6,5},{7,6},{8,7},{9,8},{10,9},{11,1... | collective-permute-start | bytes 24584 | tf_op jit(solution)/shard_map/ppermute | solution.py:110
  39.7 5.8 %collective-permute-start.6 = (bf16[16,256]{1,0:T(8,128)(2,1)S(1)}, bf16[16,256]{1,0:T(8,128)(2,1)S(1)}, u32[]{:S(2)}, u32[]{:S(2)}) collective-permute-start(bf16[16,256]{1,0:T(8,128)(2,1)S(1)} %collective-permute-done.5), channel_id=1, source_target_pairs={{0,1},{1,2},{2,3},{3,4},{4,5},{5,6},{6,7},{7,8},{8,9},{9,10},{10,1... | collective-permute-start | bytes 24584 | tf_op jit(solution)/shard_map/ppermute | solution.py:108
  39.7 5.8 %copy-start.11 = (s32[12,8]{0,1:T(8,128)S(1)}, s32[12,8]{0,1:T(8,128)}, u32[]{:S(2)}) copy-start(s32[12,8]{0,1:T(8,128)} %param.24) | copy-start | bytes 1156
  40.5 5.8 %collective-permute-start.13 = (bf16[16,256]{1,0:T(8,128)(2,1)S(1)}, bf16[16,256]{1,0:T(8,128)(2,1)S(1)}, u32[]{:S(2)}, u32[]{:S(2)}) collective-permute-start(bf16[16,256]{1,0:T(8,128)(2,1)S(1)} %collective-permute-done.12), channel_id=1, source_target_pairs={{1,0},{2,1},{3,2},{4,3},{5,4},{6,5},{7,6},{8,7},{9,8},{10,9},{11,1... | collective-permute-start | bytes 24584 | tf_op jit(solution)/shard_map/ppermute | solution.py:110
  45.5 5.8 %collective-permute-start.7 = (bf16[16,256]{1,0:T(8,128)(2,1)S(1)}, bf16[16,256]{1,0:T(8,128)(2,1)S(1)}, u32[]{:S(2)}, u32[]{:S(2)}) collective-permute-start(bf16[16,256]{1,0:T(8,128)(2,1)S(1)} %collective-permute-done.6), channel_id=1, source_target_pairs={{0,1},{1,2},{2,3},{3,4},{4,5},{5,6},{6,7},{7,8},{8,9},{9,10},{10,1... | collective-permute-start | bytes 24584 | tf_op jit(solution)/shard_map/ppermute | solution.py:108
  46.3 5.8 %collective-permute-start.14 = (bf16[16,256]{1,0:T(8,128)(2,1)S(1)}, bf16[16,256]{1,0:T(8,128)(2,1)S(1)}, u32[]{:S(2)}, u32[]{:S(2)}) collective-permute-start(bf16[16,256]{1,0:T(8,128)(2,1)S(1)} %collective-permute-done.13), channel_id=1, source_target_pairs={{1,0},{2,1},{3,2},{4,3},{5,4},{6,5},{7,6},{8,7},{9,8},{10,9},{11,1... | collective-permute-start | bytes 24584 | tf_op jit(solution)/shard_map/ppermute | solution.py:110
  52.7 0.7 copy-start.9
  60.4 1.2 copy-start.3
  61.6 160.7 %reduce-scatter.3.cloned.1.call-start = ((), (), s32[]{:S(2)}) async-start(), calls=%async_computation.2 | async-start | bytes 278528 | tf_op jit(solution)/shard_map/reduce_scatter | solution.py:154
  62.4 308.1 %all-reduce.10.cloned.1.call-start = ((), (), s32[]{:S(2)}) async-start(), calls=%async_computation.4 | async-start | bytes 1048576 | tf_op jit(solution)/shard_map/psum | solution.py:160
  159.3 1.0 copy-start.1
  196.3 24.0 %copy-start.5 = (f32[256,256]{1,0:T(8,128)S(1)}, f32[256,256]{1,0:T(8,128)}, u32[]{:S(2)}) copy-start(f32[256,256]{1,0:T(8,128)} %get-tuple-element.356) | copy-start | bytes 786436
  223.1 1.2 collective-permute-start.15
  224.3 5.2 %collective-permute-start.16 = (bf16[16,256]{1,0:T(8,128)(2,1)S(1)}, bf16[16,256]{1,0:T(8,128)(2,1)S(1)}, u32[]{:S(2)}, u32[]{:S(2)}) collective-permute-start(bf16[16,256]{1,0:T(8,128)(2,1)S(1)} %collective-permute-done.15), channel_id=1, source_target_pairs={{0,1},{1,2},{2,3},{3,4},{4,5},{5,6},{6,7},{7,8},{8,9},{9,10},{10,1... | collective-permute-start | bytes 24584 | tf_op jit(solution)/shard_map/ppermute | solution.py:108
  226.8 3.3 collective-permute-start.23
  229.5 5.8 %collective-permute-start.17 = (bf16[16,256]{1,0:T(8,128)(2,1)S(1)}, bf16[16,256]{1,0:T(8,128)(2,1)S(1)}, u32[]{:S(2)}, u32[]{:S(2)}) collective-permute-start(bf16[16,256]{1,0:T(8,128)(2,1)S(1)} %collective-permute-done.16), channel_id=1, source_target_pairs={{0,1},{1,2},{2,3},{3,4},{4,5},{5,6},{6,7},{7,8},{8,9},{9,10},{10,1... | collective-permute-start | bytes 24584 | tf_op jit(solution)/shard_map/ppermute | solution.py:108
  230.2 5.8 %collective-permute-start.24 = (bf16[16,256]{1,0:T(8,128)(2,1)S(1)}, bf16[16,256]{1,0:T(8,128)(2,1)S(1)}, u32[]{:S(2)}, u32[]{:S(2)}) collective-permute-start(bf16[16,256]{1,0:T(8,128)(2,1)S(1)} %collective-permute-done.23), channel_id=1, source_target_pairs={{1,0},{2,1},{3,2},{4,3},{5,4},{6,5},{7,6},{8,7},{9,8},{10,9},{11,1... | collective-permute-start | bytes 24584 | tf_op jit(solution)/shard_map/ppermute | solution.py:110
  235.3 5.8 %collective-permute-start.18 = (bf16[16,256]{1,0:T(8,128)(2,1)S(1)}, bf16[16,256]{1,0:T(8,128)(2,1)S(1)}, u32[]{:S(2)}, u32[]{:S(2)}) collective-permute-start(bf16[16,256]{1,0:T(8,128)(2,1)S(1)} %collective-permute-done.17), channel_id=1, source_target_pairs={{0,1},{1,2},{2,3},{3,4},{4,5},{5,6},{6,7},{7,8},{8,9},{9,10},{10,1... | collective-permute-start | bytes 24584 | tf_op jit(solution)/shard_map/ppermute | solution.py:108
  236.0 5.8 %collective-permute-start.25 = (bf16[16,256]{1,0:T(8,128)(2,1)S(1)}, bf16[16,256]{1,0:T(8,128)(2,1)S(1)}, u32[]{:S(2)}, u32[]{:S(2)}) collective-permute-start(bf16[16,256]{1,0:T(8,128)(2,1)S(1)} %collective-permute-done.24), channel_id=1, source_target_pairs={{1,0},{2,1},{3,2},{4,3},{5,4},{6,5},{7,6},{8,7},{9,8},{10,9},{11,1... | collective-permute-start | bytes 24584 | tf_op jit(solution)/shard_map/ppermute | solution.py:110
  241.1 5.8 %collective-permute-start.19 = (bf16[16,256]{1,0:T(8,128)(2,1)S(1)}, bf16[16,256]{1,0:T(8,128)(2,1)S(1)}, u32[]{:S(2)}, u32[]{:S(2)}) collective-permute-start(bf16[16,256]{1,0:T(8,128)(2,1)S(1)} %collective-permute-done.18), channel_id=1, source_target_pairs={{0,1},{1,2},{2,3},{3,4},{4,5},{5,6},{6,7},{7,8},{8,9},{9,10},{10,1... | collective-permute-start | bytes 24584 | tf_op jit(solution)/shard_map/ppermute | solution.py:108
  241.7 5.8 %collective-permute-start.26 = (bf16[16,256]{1,0:T(8,128)(2,1)S(1)}, bf16[16,256]{1,0:T(8,128)(2,1)S(1)}, u32[]{:S(2)}, u32[]{:S(2)}) collective-permute-start(bf16[16,256]{1,0:T(8,128)(2,1)S(1)} %collective-permute-done.25), channel_id=1, source_target_pairs={{1,0},{2,1},{3,2},{4,3},{5,4},{6,5},{7,6},{8,7},{9,8},{10,9},{11,1... | collective-permute-start | bytes 24584 | tf_op jit(solution)/shard_map/ppermute | solution.py:110
  246.8 5.8 %collective-permute-start.20 = (bf16[16,256]{1,0:T(8,128)(2,1)S(1)}, bf16[16,256]{1,0:T(8,128)(2,1)S(1)}, u32[]{:S(2)}, u32[]{:S(2)}) collective-permute-start(bf16[16,256]{1,0:T(8,128)(2,1)S(1)} %collective-permute-done.19), channel_id=1, source_target_pairs={{0,1},{1,2},{2,3},{3,4},{4,5},{5,6},{6,7},{7,8},{8,9},{9,10},{10,1... | collective-permute-start | bytes 24584 | tf_op jit(solution)/shard_map/ppermute | solution.py:108
  247.5 5.8 %collective-permute-start.27 = (bf16[16,256]{1,0:T(8,128)(2,1)S(1)}, bf16[16,256]{1,0:T(8,128)(2,1)S(1)}, u32[]{:S(2)}, u32[]{:S(2)}) collective-permute-start(bf16[16,256]{1,0:T(8,128)(2,1)S(1)} %collective-permute-done.26), channel_id=1, source_target_pairs={{1,0},{2,1},{3,2},{4,3},{5,4},{6,5},{7,6},{8,7},{9,8},{10,9},{11,1... | collective-permute-start | bytes 24584 | tf_op jit(solution)/shard_map/ppermute | solution.py:110
  252.6 5.8 %collective-permute-start.21 = (bf16[16,256]{1,0:T(8,128)(2,1)S(1)}, bf16[16,256]{1,0:T(8,128)(2,1)S(1)}, u32[]{:S(2)}, u32[]{:S(2)}) collective-permute-start(bf16[16,256]{1,0:T(8,128)(2,1)S(1)} %collective-permute-done.20), channel_id=1, source_target_pairs={{0,1},{1,2},{2,3},{3,4},{4,5},{5,6},{6,7},{7,8},{8,9},{9,10},{10,1... | collective-permute-start | bytes 24584 | tf_op jit(solution)/shard_map/ppermute | solution.py:108
  253.3 6.0 %collective-permute-start.28 = (bf16[16,256]{1,0:T(8,128)(2,1)S(1)}, bf16[16,256]{1,0:T(8,128)(2,1)S(1)}, u32[]{:S(2)}, u32[]{:S(2)}) collective-permute-start(bf16[16,256]{1,0:T(8,128)(2,1)S(1)} %collective-permute-done.27), channel_id=1, source_target_pairs={{1,0},{2,1},{3,2},{4,3},{5,4},{6,5},{7,6},{8,7},{9,8},{10,9},{11,1... | collective-permute-start | bytes 24584 | tf_op jit(solution)/shard_map/ppermute | solution.py:110
  258.4 6.0 %collective-permute-start.22 = (bf16[16,256]{1,0:T(8,128)(2,1)S(1)}, bf16[16,256]{1,0:T(8,128)(2,1)S(1)}, u32[]{:S(2)}, u32[]{:S(2)}) collective-permute-start(bf16[16,256]{1,0:T(8,128)(2,1)S(1)} %collective-permute-done.21), channel_id=1, source_target_pairs={{0,1},{1,2},{2,3},{3,4},{4,5},{5,6},{6,7},{7,8},{8,9},{9,10},{10,1... | collective-permute-start | bytes 24584 | tf_op jit(solution)/shard_map/ppermute | solution.py:108
  259.3 5.9 %collective-permute-start.29 = (bf16[16,256]{1,0:T(8,128)(2,1)S(1)}, bf16[16,256]{1,0:T(8,128)(2,1)S(1)}, u32[]{:S(2)}, u32[]{:S(2)}) collective-permute-start(bf16[16,256]{1,0:T(8,128)(2,1)S(1)} %collective-permute-done.28), channel_id=1, source_target_pairs={{1,0},{2,1},{3,2},{4,3},{5,4},{6,5},{7,6},{8,7},{9,8},{10,9},{11,1... | collective-permute-start | bytes 24584 | tf_op jit(solution)/shard_map/ppermute | solution.py:110
  272.9 1.2 copy-start.4
  274.1 163.2 %reduce-scatter.5.cloned.1.call-start = ((), (), s32[]{:S(2)}) async-start(), calls=%async_computation.3 | async-start | bytes 278528 | tf_op jit(solution)/shard_map/reduce_scatter | solution.py:154
  371.5 1.0 copy-start.2
  409.0 24.0 %copy-start.6 = (f32[256,256]{1,0:T(8,128)S(1)}, f32[256,256]{1,0:T(8,128)}, u32[]{:S(2)}) copy-start(f32[256,256]{1,0:T(8,128)} %get-tuple-element.354) | copy-start | bytes 786436
  (1 other events, 0.7 us)
Sparse Core Ops, SparseCore 0:
  61.7 96.5 all-reduce.11
  161.9 53.6 reduce-scatter.2
  274.3 96.1 all-reduce.9
  373.9 53.6 reduce-scatter.4
